TPU v7x, 128 devices: a whole 4x4x4 slice. The times are simulated.
128 devices in a mesh: expert: 16 (over x, y), head: 8 (over z, core).
Axes of the slice: x: 4, y: 4, z: 4, core: 2. Of those that a mesh axis runs over, the one named last changes fastest.
Arguments:
- table_cells: bfloat16 [8192, 2, 2048], P(('expert', 'head')), may hold values from -8 to 8
- w_query: bfloat16 [2048, 2048], P(None, 'head')
- w_key: bfloat16 [2048, 2048], P(None, 'head')
- w_value: bfloat16 [2048, 2048], P(None, 'head'), may hold values from -0.125 to 0.125
- w_out: bfloat16 [2048, 2048], P('head'), may hold values from -0.125 to 0.125
- norm_gain: bfloat16 [2048], replicated, may hold values from 0.099609375 to 1.8984375
- w_gate: bfloat16 [128, 704, 2048], P(('expert', 'head')), may hold values from -0.125 to 0.125
- w_up: bfloat16 [128, 704, 2048], P(('expert', 'head')), may hold values from -0.125 to 0.125
- w_down: bfloat16 [128, 704, 2048], P(('expert', 'head')), may hold values from -0.15625 to 0.15625
- lengths: int32 [2], replicated, may hold values from 2048 to 8192, as said below
- expert_of_cell: int32 [8192, 2], P(('expert', 'head')), may hold values from 0 to 63, as said below
- slot_of_cell: int32 [8192, 2], P(('expert', 'head')), may hold values from 0 to 3, as said below
Outputs:
- updated_cells: bfloat16 [8192, 2, 2048], P(('expert', 'head'))
Inputs may be any that keep to these rules, and one draw needn't show every extreme that they name: `lengths`: one table in every draw has all 8192 cells. `expert_of_cell`: within the 128 cells of one device (aligned blocks in row-major order), no expert has more than 4 cells, and in every draw one expert has exactly 4 cells in every device's block. `slot_of_cell`: cells of one device with the same expert have distinct slots.
All inputs are finite; a program needn't handle non-finite values.
Results may differ from a plain program's by a relative error of at most 0.014.
Values may be sent and summed in bfloat16 or wider, within the bound.
A program may use at most 128 MiB of HBM per device.

v0:
```python
import math
import jax
import jax.numpy as jnp
from jax import lax
from jax.sharding import PartitionSpec as P

DH = 128


def expert_half(slot_rows, gate_half, up_half, down_half):
    contract_rows = (((1,), (1,)), ((), ()))
    gate_t = lax.dot_general(
        gate_half, slot_rows, contract_rows, preferred_element_type=jnp.float32
    )
    up_t = lax.dot_general(up_half, slot_rows, contract_rows, preferred_element_type=jnp.float32)
    hidden = (jax.nn.silu(gate_t) * up_t).astype(jnp.bfloat16)
    product = lax.dot_general(
        hidden, down_half, (((0,), (0,)), ((), ())), preferred_element_type=jnp.float32
    )
    return product.astype(jnp.bfloat16)


def shards(
    table_cells,
    w_query,
    w_key,
    w_value,
    w_out,
    norm_gain,
    w_gate,
    w_up,
    w_down,
    lengths,
    expert_of_cell,
    slot_of_cell,
):
    cell_count, tables, model_width = table_cells.shape
    head_width = w_query.shape[1]
    head_count = head_width // DH
    score_scale = 1.0 / math.sqrt(DH)
    joined = jnp.concatenate([w_query, w_key, w_value], axis=1)
    shard_rows = lax.all_gather(table_cells, "head", axis=0, tiled=True)
    rows_here = shard_rows.shape[0]
    mixed_rows = jnp.dot(
        shard_rows.reshape(rows_here * tables, model_width),
        joined,
        preferred_element_type=jnp.float32,
    )
    projected = mixed_rows.astype(jnp.bfloat16).reshape(rows_here, tables, 3 * head_width)
    row_cells = projected.shape[0]
    queries = projected[:, :, :head_width].reshape(row_cells, tables, head_count, DH)
    key_rows = projected[:, :, head_width : 2 * head_width]
    value_rows = projected[:, :, 2 * head_width :]
    offset = lax.axis_index("expert") * row_cells
    own_positions = offset + jnp.arange(row_cells, dtype=jnp.int32)
    start_state = (
        jnp.full((tables, head_count, row_cells), -1e30, jnp.float32),
        jnp.zeros((tables, head_count, row_cells), jnp.float32),
        jnp.zeros((tables, head_count, row_cells, DH), jnp.float32),
    )
    key_piece = lax.all_gather(key_rows, "expert", axis=0, tiled=True)
    value_piece = lax.all_gather(value_rows, "expert", axis=0, tiled=True)
    piece_len = key_piece.shape[0]
    block_len = math.gcd(piece_len, 512)
    block_count = piece_len // block_len
    key_blocks = key_piece.reshape(block_count, block_len, tables, head_count, DH)
    value_blocks = value_piece.reshape(block_count, block_len, tables, head_count, DH)
    block_starts = jnp.arange(block_count, dtype=jnp.int32) * block_len

    def step(carried, block_item):
        running_max, running_sum, accum = carried
        key_block, value_block, block_first = block_item
        scores = (
            jnp.einsum("qshd,kshd->shqk", queries, key_block, preferred_element_type=jnp.float32)
            * score_scale
        )
        key_valid = (block_first + jnp.arange(block_len, dtype=jnp.int32))[None, :] < lengths[
            :, None
        ]
        scores = jnp.where(key_valid[:, None, None, :], scores, -jnp.inf)
        new_max = jnp.maximum(running_max, jnp.max(scores, axis=-1))
        factor = jnp.exp(running_max - new_max)
        exp_scores = jnp.exp(scores - new_max[..., None])
        running_sum = running_sum * factor + jnp.sum(exp_scores, axis=-1)
        accum = accum * factor[..., None] + jnp.einsum(
            "shqk,kshd->shqd",
            exp_scores.astype(jnp.bfloat16),
            value_block,
            preferred_element_type=jnp.float32,
        )
        return ((new_max, running_sum, accum), None)

    finished, _ = lax.scan(step, start_state, (key_blocks, value_blocks, block_starts))
    running_max, running_sum, accum = finished
    normalized = accum / running_sum[..., None]
    live = own_positions[None, :] < lengths[:, None]
    normalized = jnp.where(live[:, None, :, None], normalized, 0.0)
    attended = (
        jnp.transpose(normalized, (2, 0, 1, 3))
        .reshape(row_cells, tables, head_width)
        .astype(jnp.bfloat16)
    )
    count_rows = cell_count * lax.axis_size("head")
    product = jnp.dot(
        attended.reshape(count_rows * tables, head_width), w_out, preferred_element_type=jnp.float32
    )
    summed = lax.psum_scatter(
        product.reshape(count_rows, tables, model_width).astype(jnp.bfloat16),
        "head",
        scatter_dimension=0,
        tiled=True,
    ).astype(jnp.float32)
    residual = table_cells.astype(jnp.float32) + summed
    mean_square = jnp.mean(residual * residual, axis=-1, keepdims=True)
    normed = (residual * lax.rsqrt(mean_square + 1e-06) * norm_gain.astype(jnp.float32)).astype(
        jnp.bfloat16
    )
    rows_dev = cell_count * tables
    normed_rows = normed.reshape(rows_dev, model_width)
    expert_count = lax.axis_size("expert") * lax.axis_size("head") // 2
    slot_cap = 2 * max(1, rows_dev // expert_count)
    target = expert_of_cell.reshape(rows_dev) * slot_cap + slot_of_cell.reshape(rows_dev)
    slot_table = (
        jnp.arange(expert_count * slot_cap, dtype=jnp.int32)[:, None] == target[None, :]
    ).astype(jnp.bfloat16)
    send_rows = jnp.dot(slot_table, normed_rows, preferred_element_type=jnp.float32).astype(
        jnp.bfloat16
    )
    gate_half = w_gate[0]
    up_half = w_up[0]
    down_half = w_down[0]
    doubled = jnp.repeat(send_rows.reshape(expert_count, slot_cap, model_width), 2, axis=0)
    received = lax.all_to_all(doubled, ("expert", "head"), split_axis=0, concat_axis=0, tiled=True)
    sources = received.shape[0]
    item_count = received.shape[1]
    flat_rows = received.reshape(sources * item_count, model_width)
    gathered = lax.all_to_all(
        expert_half(flat_rows, gate_half, up_half, down_half).reshape(
            sources, item_count, model_width
        ),
        ("expert", "head"),
        split_axis=0,
        concat_axis=0,
        tiled=True,
    )
    halves = gathered.reshape(expert_count, 2, slot_cap, model_width).astype(jnp.float32)
    combined = (
        (halves[:, 0] + halves[:, 1])
        .astype(jnp.bfloat16)
        .reshape(expert_count * slot_cap, model_width)
    )
    expert_out = lax.dot_general(
        slot_table, combined, (((0,), (0,)), ((), ())), preferred_element_type=jnp.float32
    )
    updated = (residual.reshape(rows_dev, model_width) + expert_out).astype(jnp.bfloat16)
    return updated.reshape(cell_count, tables, model_width)


def solution(mesh):
    placed = (
        P(("expert", "head"), None, None),
        P(None, "head"),
        P(None, "head"),
        P(None, "head"),
        P("head", None),
        P(),
        P(("expert", "head"), None, None),
        P(("expert", "head"), None, None),
        P(("expert", "head"), None, None),
        P(),
        P(("expert", "head"), None),
        P(("expert", "head"), None),
    )
    return jax.shard_map(
        shards,
        mesh=mesh,
        in_specs=placed,
        out_specs=P(("expert", "head"), None, None),
        check_vma=False,
    )
```

profile of v0, /device:TPU:1, one launch (start us, length us, event | category | flops | bytes accessed | tf_op | source)
XLA Modules:
  0.0 631.7 jit_solution(11269988385761301558)
XLA Ops:
  7.3 37.8 %all-gather.4.cloned.1.call-done = bf16[512,2,2048]{2,1,0:T(2,128)(2,1)} async-done(((bf16[64,2,2048]{2,1,0:T(2,128)(2,1)}), bf16[512,2,2048]{2,1,0:T(2,128)(2,1)}) %all-gather.4.cloned.1.call-update) | async-done | bytes 4194320 | tf_op jit(solution)/shard_map/all_gather | solution.py:42
  45.1 7.2 %reshape.135 = bf16[1024,2048]{1,0:T(8,128)(2,1)} reshape(bf16[512,2,2048]{2,1,0:T(2,128)(2,1)} %all-gather.4.cloned.1.call-done) | data formatting | bytes 8388608 | tf_op jit(solution)/shard_map/reshape | solution.py:45
  52.3 7.8 %fusion.33 = bf16[1024,768]{0,1:T(8,128)(2,1)} fusion(bf16[1024,2048]{1,0:T(8,128)(2,1)} %reshape.135, bf16[2048,256]{1,0:T(8,128)(2,1)} %param.17, bf16[2048,256]{1,0:T(8,128)(2,1)} %param.16, bf16[2048,256]{1,0:T(8,128)(2,1)} %param.15), kind=kOutput, calls=%fused_computation.46 | convolution fusion | flops 3231449088 | bytes 8912896 | tf_op jit(solution)/shard_map/dot_general | solution.py:44
  62.7 4.5 reshape.136
  67.2 3.4 fusion.56
  74.5 66.3 %all-gather.6.cloned.1.call-done = bf16[8192,2,256]{2,1,0:T(2,128)(2,1)} async-done(((bf16[512,2,256]{2,1,0:T(2,128)(2,1)}), bf16[8192,2,256]{2,1,0:T(2,128)(2,1)}) %all-gather.6.cloned.1.call-update) | async-done | bytes 8388624 | tf_op jit(solution)/shard_map/all_gather | solution.py:61
  140.8 21.6 %reshape.149 = bf16[16,512,2,2,128]{4,3,2,1,0:T(2,128)(2,1)} reshape(bf16[8192,2,256]{2,1,0:T(2,128)(2,1)} %all-gather.6.cloned.1.call-done) | data formatting | bytes 16777216 | tf_op jit(solution)/shard_map/reshape | solution.py:66
  162.5 50.9 %all-gather.8.cloned.1.call-done = bf16[8192,2,256]{2,1,0:T(2,128)(2,1)} async-done(((bf16[512,2,256]{2,1,0:T(2,128)(2,1)}), bf16[8192,2,256]{2,1,0:T(2,128)(2,1)}) %all-gather.8.cloned.1.call-update) | async-done | bytes 8388624 | tf_op jit(solution)/shard_map/all_gather | solution.py:62
  213.3 21.6 %reshape.150 = bf16[16,512,2,2,128]{4,3,2,1,0:T(2,128)(2,1)} reshape(bf16[8192,2,256]{2,1,0:T(2,128)(2,1)} %all-gather.8.cloned.1.call-done) | data formatting | bytes 16777216 | tf_op jit(solution)/shard_map/reshape | solution.py:67
  234.9 227.6 %while.15 = (s32[]{:T(128)}, f32[2,2,512]{2,1,0:T(2,128)S(1)}, f32[2,2,512]{2,1,0:T(2,128)S(1)}, f32[2,2,512,128]{3,2,1,0:T(8,128)}, s32[16]{0:T(128)S(1)}, /*in...) while((s32[]{:T(128)}, f32[2,2,512]{2,1,0:T(2,128)S(1)}, ...), condition=%wide.region_3.4_spmd.clone, body=%wide.region_0.3_spmd.clone.sunk | while | flops 549203456 | bytes 35266736 | solution.py:93
  241.6 3.3 fusion.73
  245.1 3.8 fusion.75
  255.5 3.3 fusion.73
  259.0 4.1 fusion.75
  269.8 3.3 fusion.73
  273.2 4.1 fusion.75
  284.0 3.3 fusion.73
  287.5 4.1 fusion.75
  298.3 3.3 fusion.73
  301.7 4.1 fusion.75
  312.5 3.3 fusion.73
  316.0 4.1 fusion.75
  326.8 3.3 fusion.73
  330.2 4.1 fusion.75
  341.0 3.3 fusion.73
  344.5 4.1 fusion.75
  355.3 3.3 fusion.73
  358.7 4.1 fusion.75
  373.0 4.1 fusion.75
  383.8 3.3 fusion.73
  387.2 4.1 fusion.75
  401.5 4.1 fusion.75
  415.7 4.1 fusion.75
  426.5 3.3 fusion.73
  430.0 4.1 fusion.75
  440.8 3.3 fusion.73
  444.2 4.1 fusion.75
  455.0 3.3 fusion.73
  458.5 4.1 fusion.75
  466.5 4.5 convolution_convert_fusion
  471.9 34.2 %reduce-scatter.2.cloned.1.call-done = bf16[64,2,2048]{2,0,1:T(8,128)(2,1)} async-done(((bf16[512,2,2048]{2,0,1:T(8,128)(2,1)}), bf16[64,2,2048]{2,0,1:T(8,128)(2,1)}) %reduce-scatter.2.cloned.1.call-update) | async-done | bytes 524304 | tf_op jit(solution)/shard_map/reduce_scatter | solution.py:107
  518.5 40.4 %all_to_all.10 = bf16[128,4,2048]{2,1,0:T(4,128)(2,1)} all-to-all(bf16[128,4,2048]{2,1,0:T(4,128)(2,1)S(1)} %bitcast.83), channel_id=1, replica_groups=mesh['expert'=16,'head'=8] {'expert','head'}, dimensions={0} | all-to-all | bytes 4194304 | tf_op jit(solution)/shard_map/all_to_all | solution.py:133
  558.9 4.0 reshape.144
  562.9 5.3 fusion.36
  568.1 7.6 %convolution_convert_fusion.1 = bf16[512,2048]{1,0:T(8,128)(2,1)} fusion(bf16[1,704,2048]{2,1,0:T(8,128)(2,1)S(1)} %copy-done, bf16[512,2048]{1,0:T(8,128)(2,1)} %reshape.144, bf16[1,704,2048]{2,1,0:T(8,128)(2,1)} %param.21, f32[704,512]{1,0:T(8,128)} %fusion.36), kind=kOutput, calls=%fused_computation.34 | convolution fusion | flops 2956001280 | bytes 11403264 | tf_op jit(solution)/shard_map/dot_general | solution.py:17
  575.8 4.1 reshape.145
  579.9 5.7 all-to-all-start.1
  591.5 24.4 %all-to-all-done.1 = bf16[128,4,2048]{2,1,0:T(4,128)(2,1)} async-done(((bf16[128,4,2048]{2,1,0:T(4,128)(2,1)}), bf16[128,4,2048]{2,1,0:T(4,128)(2,1)}, u32[]{:S(2)}, u32[]{:S(2)}) %all-to-all-start.1) | async-done | bytes 2097184 | tf_op jit(solution)/shard_map/all_to_all | solution.py:137
  (213 shorter events, 159.2 us)
Async XLA Ops:
  6.5 561.6 %copy-start = (bf16[1,704,2048]{2,1,0:T(8,128)(2,1)S(1)}, bf16[1,704,2048]{2,1,0:T(8,128)(2,1)}, u32[]{:S(2)}) copy-start(bf16[1,704,2048]{2,1,0:T(8,128)(2,1)} %param.22) | copy-start | bytes 8650756
  6.5 38.5 %all-gather.4.cloned.1.call-start = ((), (), s32[]{:S(2)}) async-start(), calls=%async_computation.3 | async-start | bytes 4718592 | tf_op jit(solution)/shard_map/all_gather | solution.py:42
  7.3 133.5 %all-gather.6.cloned.1.call-start = ((), (), s32[]{:S(2)}) async-start(), calls=%async_computation.4 | async-start | bytes 8912896 | tf_op jit(solution)/shard_map/all_gather | solution.py:61
  62.7 9.0 %copy-start.3 = (s32[2]{0:T(128)S(1)}, s32[2]{0:T(128)}, u32[]{:S(2)}) copy-start(s32[2]{0:T(128)} %param.23) | copy-start | bytes 28
  70.7 142.7 %all-gather.8.cloned.1.call-start = ((), (), s32[]{:S(2)}) async-start(), calls=%async_computation.5 | async-start | bytes 8912896 | tf_op jit(solution)/shard_map/all_gather | solution.py:62
  71.4 434.7 %reduce-scatter.2.cloned.1.call-start = ((), (), s32[]{:S(2)}) async-start(), calls=%async_computation.6 | async-start | bytes 4718592 | tf_op jit(solution)/shard_map/reduce_scatter | solution.py:107
  241.6 3.4 copy-start.1
  255.5 3.4 copy-start.1
  269.8 3.4 copy-start.1
  284.0 3.4 copy-start.1
  298.3 3.4 copy-start.1
  312.5 3.4 copy-start.1
  326.8 3.4 copy-start.1
  341.0 3.4 copy-start.1
  355.3 3.4 copy-start.1
  369.5 3.4 copy-start.1
  383.8 3.4 copy-start.1
  398.0 3.4 copy-start.1
  412.3 3.4 copy-start.1
  426.5 3.4 copy-start.1
  440.8 3.4 copy-start.1
  455.0 3.4 copy-start.1
  471.0 0.7 copy-start.4
  471.0 0.7 copy-start.5
  471.0 0.7 copy-start.6
  471.0 35.2 %copy-start.2 = (bf16[64,2,2048]{2,1,0:T(2,128)(2,1)S(1)}, bf16[64,2,2048]{2,1,0:T(2,128)(2,1)}, u32[]{:S(2)}) copy-start(bf16[64,2,2048]{2,1,0:T(2,128)(2,1)} %param.14) | copy-start | bytes 1572868
  579.9 36.0 %all-to-all-start.1 = ((bf16[128,4,2048]{2,1,0:T(4,128)(2,1)}), bf16[128,4,2048]{2,1,0:T(4,128)(2,1)}, u32[]{:S(2)}, u32[]{:S(2)}) async-start(bf16[128,4,2048]{2,1,0:T(4,128)(2,1)} %reshape.145), calls=%async_computation.2 | async-start | bytes 4194304 | tf_op jit(solution)/shard_map/all_to_all | solution.py:137
Sparse Core Ops, SparseCore 0:
  9.1 35.9 all-gather.3
  70.8 69.9 all-gather.5
  143.0 70.3 all-gather.7
  471.1 34.9 reduce-scatter.1
where the time goes:
time: 635 us; the launch traced here: 632 us
  waiting for transfers between devices  215 us (34%)
  local copies, waits for them, and re-layouts  146 us (23%)
  matrix products  138 us (22%)
  other arithmetic  73.5 us (12%)
  blocking collectives  40.4 us (6%)
  between operations  13.2 us (2%)
    all_gather x1, waiting for transfers between devices, shards(): key_piece = lax.all_gather(key_rows, 'expert', axis=0, tiled=True)  66.3 us
    dot_general x16, matrix products, step(): jnp.einsum('shqk,kshd->shqd', exp_scores.astype(jnp.bfloat16), value_bloc...  65.2 us
    dynamic_slice x32, local copies, waits for them, and re-layouts, shards(): lax.scan(step, start_state, (key_blocks, value_blocks, block_starts))  52.7 us
    reduce_sum x16, other arithmetic, step(): running_sum = running_sum * factor + jnp.sum(exp_scores, axis=-1)  52.1 us
    all_gather x1, waiting for transfers between devices, shards(): value_piece = lax.all_gather(value_rows, 'expert', axis=0, tiled=True)  50.9 us
    dot_general x16, matrix products, step(): jnp.einsum('qshd,kshd->shqk', queries, key_block, preferred_element_type=...  42.8 us
    all_to_all x1, blocking collectives, shards(): lax.all_to_all(doubled, ('expert', 'head'), split_axis=0, concat_axis=0,...  40.4 us
    all_gather x1, waiting for transfers between devices, shards(): shard_rows = lax.all_gather(table_cells, 'head', axis=0, tiled=True)  37.8 us
  transfers between devices with their start and end apart: 5, of which 5 were waited for; matrix products, arithmetic and copies ran while one was open for 5% of the time, Pallas kernels for 0%

commit v1 on v0

--- a/solution.py
+++ b/solution.py
@@ -39,7 +39,24 @@
     head_count = head_width // DH
     score_scale = 1.0 / math.sqrt(DH)
     joined = jnp.concatenate([w_query, w_key, w_value], axis=1)
-    shard_rows = lax.all_gather(table_cells, "head", axis=0, tiled=True)
+    size, place, rows = (lax.axis_size("head"), lax.axis_index("head"), table_cells.shape[0])
+    right = [(i, (i + 1) % size) for i in range(size)]
+    left = [(i, (i - 1) % size) for i in range(size)]
+    out = jnp.zeros(
+        (*table_cells.shape[:0], size * rows, *table_cells.shape[0 + 1 :]), table_cells.dtype
+    )
+    out = lax.dynamic_update_slice_in_dim(out, table_cells, place * rows, axis=0)
+    from_left = from_right = table_cells
+    half = size // 2
+    for hop in range(1, half + 1):
+        from_left = lax.ppermute(from_left, "head", right)
+        out = lax.dynamic_update_slice_in_dim(out, from_left, (place - hop) % size * rows, axis=0)
+        if hop < size - half:
+            from_right = lax.ppermute(from_right, "head", left)
+            out = lax.dynamic_update_slice_in_dim(
+                out, from_right, (place + hop) % size * rows, axis=0
+            )
+    shard_rows = out
     rows_here = shard_rows.shape[0]
     mixed_rows = jnp.dot(
         shard_rows.reshape(rows_here * tables, model_width),

time: 635 us -> 638 us (level); the launches traced: 632 us -> 626 us
  local copies, waits for them, and re-layouts: 146 us -> 129 us
  waiting for transfers between devices: 215 us -> 199 us
  matrix products: 138 us -> 153 us
  starting transfers between devices: 5.97 us -> 16.6 us
    unnamed x13 -> x22, local copies, waits for them, and re-layouts: 2 us -> 58.1 us
    dynamic_slice x32 -> x16, local copies, waits for them, and re-layouts: 52.7 us -> 9.32 us  [shards(): lax.scan(step, start_state, (key_blocks, value_blocks, block_starts))]
    reshape x2 -> x0, local copies, waits for them, and re-layouts: 43.3 us -> none  [the longest x1 21.6 us: shards(): key_piece.reshape(block_count, block_len, tables, head_count, DH)]
    all_gather x1 -> x0, waiting for transfers between devices: 37.8 us -> none  [shards(): shard_rows = lax.all_gather(table_cells, 'head', axis=0, tiled=True)]
    dot_general x16, matrix products: 42.8 us -> 59.3 us  [step(): jnp.einsum('qshd,kshd->shqk', queries, key_block, preferred_element_type=...]
    dynamic_update_slice x0 -> x8, local copies, waits for them, and re-layouts: none -> 13.5 us  [the longest x4 6.74 us: shards(): lax.dynamic_update_slice_in_dim(out, from_left, (place - hop) % size * ro...]
    ppermute x0 -> x7, starting transfers between devices: none -> 10.4 us  [the longest x4 8.66 us: shards(): from_left = lax.ppermute(from_left, 'head', right)]
    all_gather x1, waiting for transfers between devices: 66.3 us -> 76.6 us  [shards(): key_piece = lax.all_gather(key_rows, 'expert', axis=0, tiled=True)]
  transfers between devices with their start and end apart: 5 -> 11, of which waited for: 5 -> 8; matrix products, arithmetic and copies ran while one was open for 5% -> 8% of each run, Pallas kernels for 0% -> 0%
where the time goes in v1:
time: 638 us; the launch traced here: 626 us
  waiting for transfers between devices  199 us (31%)
  matrix products  153 us (24%)
  local copies, waits for them, and re-layouts  129 us (20%)
  other arithmetic  73.5 us (12%)
  blocking collectives  40.5 us (6%)
  starting transfers between devices  16.6 us (3%)
  between operations  13.5 us (2%)
    all_gather x1, waiting for transfers between devices, shards(): key_piece = lax.all_gather(key_rows, 'expert', axis=0, tiled=True)  76.6 us
    dot_general x16, matrix products, step(): jnp.einsum('shqk,kshd->shqd', exp_scores.astype(jnp.bfloat16), value_bloc...  64.6 us
    dot_general x16, matrix products, step(): jnp.einsum('qshd,kshd->shqk', queries, key_block, preferred_element_type=...  59.3 us
    unnamed x22, local copies, waits for them, and re-layouts  58.1 us
    all_gather x1, waiting for transfers between devices, shards(): value_piece = lax.all_gather(value_rows, 'expert', axis=0, tiled=True)  54.1 us
    reduce_sum x16, other arithmetic, step(): running_sum = running_sum * factor + jnp.sum(exp_scores, axis=-1)  52.1 us
    all_to_all x1, blocking collectives, shards(): lax.all_to_all(doubled, ('expert', 'head'), split_axis=0, concat_axis=0,...  40.5 us
    reduce_scatter x1, waiting for transfers between devices, shards(): lax.psum_scatter(product.reshape(count_rows, tables, model_width).astype(...  35.4 us
  transfers between devices with their start and end apart: 11, of which 8 were waited for; matrix products, arithmetic and copies ran while one was open for 8% of the time, Pallas kernels for 0%

profile of v1, /device:TPU:1, one launch (start us, length us, event | category | flops | bytes accessed | tf_op | source)
XLA Modules:
  0.0 626.4 jit_solution(13407108045165710774)
XLA Ops:
  9.6 6.4 %collective-permute-done = bf16[64,2,2048]{2,1,0:T(2,128)(2,1)} collective-permute-done((bf16[64,2,2048]{2,1,0:T(2,128)(2,1)}, bf16[64,2,2048]{2,1,0:T(2,128)(2,1)}, u32[]{:S(2)}, u32[]{:S(2)}) %collective-permute-start) | collective-permute-done | bytes 524320 | tf_op jit(solution)/shard_map/ppermute | solution.py:52
  18.7 4.1 broadcast_in_dim.54
  43.5 7.2 %reshape.135 = bf16[1024,2048]{1,0:T(8,128)(2,1)} reshape(bf16[512,2,2048]{2,1,0:T(2,128)(2,1)} %constant_dynamic-update-slice_fusion) | data formatting | bytes 8388608 | tf_op jit(solution)/shard_map/reshape | solution.py:62
  50.7 7.7 %fusion.36 = bf16[1024,768]{1,0:T(8,128)(2,1)} fusion(bf16[1024,2048]{1,0:T(8,128)(2,1)} %reshape.135, bf16[2048,256]{1,0:T(8,128)(2,1)} %param.17, bf16[2048,256]{1,0:T(8,128)(2,1)} %param.16, bf16[2048,256]{1,0:T(8,128)(2,1)} %param.15), kind=kOutput, calls=%fused_computation.47 | convolution fusion | flops 3231449088 | bytes 8912896 | tf_op jit(solution)/shard_map/dot_general | solution.py:61
  58.4 4.5 reshape.136
  73.9 76.6 %all-gather.3.cloned.1.call-done = bf16[8192,2,256]{0,2,1:T(8,128)(2,1)} async-done(((bf16[512,2,256]{0,2,1:T(8,128)(2,1)}), bf16[8192,2,256]{0,2,1:T(8,128)(2,1)}) %all-gather.3.cloned.1.call-update) | async-done | bytes 8388624 | tf_op jit(solution)/shard_map/all_gather | solution.py:78
  150.5 11.0 %copy.34 = bf16[64,8,16,512]{3,2,1,0:T(8,128)(2,1)} copy(bf16[64,8,16,512]{3,1,2,0:T(8,128)(2,1)} %bitcast.95) | data formatting | bytes 16777216
  161.5 14.7 %copy.21 = bf16[16,512,2,2,128]{4,1,3,2,0:T(8,128)(2,1)} copy(bf16[16,512,2,2,128]{1,0,4,3,2:T(8,128)(2,1)} %bitcast.93) | data formatting | bytes 16777216
  176.2 54.1 %all-gather.5.cloned.1.call-done = bf16[8192,2,256]{0,2,1:T(8,128)(2,1)} async-done(((bf16[512,2,256]{0,2,1:T(8,128)(2,1)}), bf16[8192,2,256]{0,2,1:T(8,128)(2,1)}) %all-gather.5.cloned.1.call-update) | async-done | bytes 8388624 | tf_op jit(solution)/shard_map/all_gather | solution.py:79
  230.3 11.0 %copy.35 = bf16[64,8,16,512]{3,2,1,0:T(8,128)(2,1)} copy(bf16[64,8,16,512]{3,1,2,0:T(8,128)(2,1)} %bitcast.96) | data formatting | bytes 16777216
  241.3 14.6 %copy.23 = bf16[16,512,2,2,128]{4,1,3,2,0:T(8,128)(2,1)} copy(bf16[16,512,2,2,128]{1,0,4,3,2:T(8,128)(2,1)} %bitcast.94) | data formatting | bytes 16777216
  255.9 200.3 %while.15 = (s32[]{:T(128)}, f32[2,2,512]{2,1,0:T(2,128)S(1)}, f32[2,2,512]{2,1,0:T(2,128)S(1)}, f32[2,2,512,128]{3,2,1,0:T(8,128)}, s32[16]{0:T(128)S(1)}, /*in...) while((s32[]{:T(128)}, f32[2,2,512]{2,1,0:T(2,128)S(1)}, ...), condition=%wide.region_3.4_spmd.clone, body=%wide.region_0.3_spmd.clone.sunk | while | flops 549203456 | bytes 33170604 | solution.py:110
  264.5 3.7 fusion.80
  269.6 3.7 bitcast_reduce_fusion.2
  276.7 4.1 fusion.80
  282.1 3.7 bitcast_reduce_fusion.2
  289.3 4.1 fusion.80
  294.6 3.7 bitcast_reduce_fusion.2
  301.8 4.1 fusion.80
  307.2 3.7 bitcast_reduce_fusion.2
  314.3 4.1 fusion.80
  326.8 4.1 fusion.80
  332.2 3.7 bitcast_reduce_fusion.2
  339.4 4.1 fusion.80
  344.7 3.7 bitcast_reduce_fusion.2
  351.9 4.1 fusion.80
  357.3 3.7 bitcast_reduce_fusion.2
  364.4 4.1 fusion.80
  369.8 3.7 bitcast_reduce_fusion.2
  377.0 4.1 fusion.80
  389.5 4.1 fusion.80
  394.9 3.7 bitcast_reduce_fusion.2
  402.0 4.1 fusion.80
  414.5 4.1 fusion.80
  419.9 3.7 bitcast_reduce_fusion.2
  427.1 4.1 fusion.80
  432.4 3.7 bitcast_reduce_fusion.2
  439.6 4.1 fusion.80
  452.1 4.1 fusion.80
  460.1 4.5 convolution_convert_fusion
  465.0 35.4 %reduce-scatter.2.cloned.1.call-done = bf16[64,2,2048]{2,0,1:T(8,128)(2,1)} async-done(((bf16[512,2,2048]{2,0,1:T(8,128)(2,1)}), bf16[64,2,2048]{2,0,1:T(8,128)(2,1)}) %reduce-scatter.2.cloned.1.call-update) | async-done | bytes 524304 | tf_op jit(solution)/shard_map/reduce_scatter | solution.py:124
  512.8 40.5 %all_to_all.10 = bf16[128,4,2048]{2,1,0:T(4,128)(2,1)} all-to-all(bf16[128,4,2048]{2,1,0:T(4,128)(2,1)S(1)} %bitcast.97), channel_id=1, replica_groups=mesh['expert'=16,'head'=8] {'expert','head'}, dimensions={0} | all-to-all | bytes 4194304 | tf_op jit(solution)/shard_map/all_to_all | solution.py:150
  553.4 4.0 reshape.144
  557.4 5.3 fusion.39
  562.6 7.6 %convolution_convert_fusion.1 = bf16[512,2048]{1,0:T(8,128)(2,1)} fusion(bf16[1,704,2048]{2,1,0:T(8,128)(2,1)S(1)} %copy-done, bf16[512,2048]{1,0:T(8,128)(2,1)} %reshape.144, bf16[1,704,2048]{2,1,0:T(8,128)(2,1)} %param.21, f32[704,512]{1,0:T(8,128)} %fusion.39), kind=kOutput, calls=%fused_computation.36 | convolution fusion | flops 2956001280 | bytes 11403264 | tf_op jit(solution)/shard_map/dot_general | solution.py:17
  570.3 4.1 reshape.145
  574.4 5.7 all-to-all-start.1
  586.0 24.4 %all-to-all-done.1 = bf16[128,4,2048]{2,1,0:T(4,128)(2,1)} async-done(((bf16[128,4,2048]{2,1,0:T(4,128)(2,1)}), bf16[128,4,2048]{2,1,0:T(4,128)(2,1)}, u32[]{:S(2)}, u32[]{:S(2)}) %all-to-all-start.1) | async-done | bytes 2097184 | tf_op jit(solution)/shard_map/all_to_all | solution.py:154
  (222 shorter events, 163.4 us)
Async XLA Ops:
  6.5 556.1 %copy-start = (bf16[1,704,2048]{2,1,0:T(8,128)(2,1)S(1)}, bf16[1,704,2048]{2,1,0:T(8,128)(2,1)}, u32[]{:S(2)}) copy-start(bf16[1,704,2048]{2,1,0:T(8,128)(2,1)} %param.22) | copy-start | bytes 8650756
  6.5 16.3 %copy-start.2 = (bf16[64,2,2048]{2,1,0:T(2,128)(2,1)S(1)}, bf16[64,2,2048]{2,1,0:T(2,128)(2,1)}, u32[]{:S(2)}) copy-start(bf16[64,2,2048]{2,1,0:T(2,128)(2,1)} %param.14) | copy-start | bytes 1572868
  6.5 144.0 %all-gather.3.cloned.1.call-start = ((), (), s32[]{:S(2)}) async-start(), calls=%async_computation.3 | async-start | bytes 8912896 | tf_op jit(solution)/shard_map/all_gather | solution.py:78
  6.5 9.5 %collective-permute-start = (bf16[64,2,2048]{2,1,0:T(2,128)(2,1)}, bf16[64,2,2048]{2,1,0:T(2,128)(2,1)}, u32[]{:S(2)}, u32[]{:S(2)}) collective-permute-start(bf16[64,2,2048]{2,1,0:T(2,128)(2,1)} %param.14), channel_id=1, source_target_pairs={{0,1},{1,2},{2,3},{3,4},{4,5},{5,6},{6,7},{7,0},{8,9},{9,10},{10,1... | collective-permute-start | bytes 1572872 | tf_op jit(solution)/shard_map/ppermute | solution.py:52
  9.6 8.9 %collective-permute-start.1 = (bf16[64,2,2048]{2,1,0:T(2,128)(2,1)}, bf16[64,2,2048]{2,1,0:T(2,128)(2,1)}, u32[]{:S(2)}, u32[]{:S(2)}) collective-permute-start(bf16[64,2,2048]{2,1,0:T(2,128)(2,1)} %param.14), channel_id=1, source_target_pairs={{0,7},{1,0},{2,1},{3,2},{4,3},{5,4},{6,5},{7,6},{8,15},{9,8},{10,9... | collective-permute-start | bytes 1572872 | tf_op jit(solution)/shard_map/ppermute | solution.py:55
  16.0 8.9 %collective-permute-start.2 = (bf16[64,2,2048]{2,1,0:T(2,128)(2,1)}, bf16[64,2,2048]{2,1,0:T(2,128)(2,1)}, u32[]{:S(2)}, u32[]{:S(2)}) collective-permute-start(bf16[64,2,2048]{2,1,0:T(2,128)(2,1)} %collective-permute-done), channel_id=1, source_target_pairs={{0,1},{1,2},{2,3},{3,4},{4,5},{5,6},{6,7},{7,0},{8,9},{9,10},{10,1... | collective-permute-start | bytes 1572872 | tf_op jit(solution)/shard_map/ppermute | solution.py:52
  18.5 13.4 %collective-permute-start.3 = (bf16[64,2,2048]{2,1,0:T(2,128)(2,1)}, bf16[64,2,2048]{2,1,0:T(2,128)(2,1)}, u32[]{:S(2)}, u32[]{:S(2)}) collective-permute-start(bf16[64,2,2048]{2,1,0:T(2,128)(2,1)} %collective-permute-done.1), channel_id=1, source_target_pairs={{0,7},{1,0},{2,1},{3,2},{4,3},{5,4},{6,5},{7,6},{8,15},{9,8},{10,9... | collective-permute-start | bytes 1572872 | tf_op jit(solution)/shard_map/ppermute | solution.py:55
  24.9 10.6 %collective-permute-start.4 = (bf16[64,2,2048]{2,1,0:T(2,128)(2,1)}, bf16[64,2,2048]{2,1,0:T(2,128)(2,1)S(1)}, u32[]{:S(2)}, u32[]{:S(2)}) collective-permute-start(bf16[64,2,2048]{2,1,0:T(2,128)(2,1)} %collective-permute-done.2), channel_id=1, source_target_pairs={{0,1},{1,2},{2,3},{3,4},{4,5},{5,6},{6,7},{7,0},{8,9},{9,10},{10,1... | collective-permute-start | bytes 1572872 | tf_op jit(solution)/shard_map/ppermute | solution.py:52
  31.8 8.8 %collective-permute-start.5 = (bf16[64,2,2048]{2,1,0:T(2,128)(2,1)}, bf16[64,2,2048]{2,1,0:T(2,128)(2,1)S(1)}, u32[]{:S(2)}, u32[]{:S(2)}) collective-permute-start(bf16[64,2,2048]{2,1,0:T(2,128)(2,1)} %collective-permute-done.3), channel_id=1, source_target_pairs={{0,7},{1,0},{2,1},{3,2},{4,3},{5,4},{6,5},{7,6},{8,15},{9,8},{10,9... | collective-permute-start | bytes 1572872 | tf_op jit(solution)/shard_map/ppermute | solution.py:55
  35.6 6.8 %collective-permute-start.6 = (bf16[64,2,2048]{2,1,0:T(2,128)(2,1)S(1)}, bf16[64,2,2048]{2,1,0:T(2,128)(2,1)S(1)}, u32[]{:S(2)}, u32[]{:S(2)}) collective-permute-start(bf16[64,2,2048]{2,1,0:T(2,128)(2,1)S(1)} %collective-permute-done.4), channel_id=1, source_target_pairs={{0,1},{1,2},{2,3},{3,4},{4,5},{5,6},{6,7},{7,0},{8,9},{9,10},{10,1... | collective-permute-start | bytes 1572872 | tf_op jit(solution)/shard_map/ppermute | solution.py:52
  58.4 12.6 %copy-start.4 = (s32[2]{0:T(128)S(1)}, s32[2]{0:T(128)}, u32[]{:S(2)}) copy-start(s32[2]{0:T(128)} %param.23) | copy-start | bytes 28
  68.4 161.9 %all-gather.5.cloned.1.call-start = ((), (), s32[]{:S(2)}) async-start(), calls=%async_computation.4 | async-start | bytes 8912896 | tf_op jit(solution)/shard_map/all_gather | solution.py:79
  70.5 429.9 %reduce-scatter.2.cloned.1.call-start = ((), (), s32[]{:S(2)}) async-start(), calls=%async_computation.5 | async-start | bytes 4718592 | tf_op jit(solution)/shard_map/reduce_scatter | solution.py:124
  261.1 3.4 copy-start.1
  273.3 3.4 copy-start.1
  285.8 3.4 copy-start.1
  298.3 3.4 copy-start.1
  310.9 3.4 copy-start.1
  323.4 3.4 copy-start.1
  335.9 3.4 copy-start.1
  348.5 3.4 copy-start.1
  361.0 3.4 copy-start.1
  373.5 3.4 copy-start.1
  386.0 3.4 copy-start.1
  398.6 3.4 copy-start.1
  411.1 3.4 copy-start.1
  423.6 3.4 copy-start.1
  436.2 3.4 copy-start.1
  448.7 3.4 copy-start.1
  460.1 4.6 copy-start.5
  460.1 4.6 copy-start.6
  460.1 4.6 copy-start.7
  460.1 40.3 %copy-start.3 = (bf16[64,2,2048]{2,1,0:T(2,128)(2,1)S(1)}, bf16[64,2,2048]{2,1,0:T(2,128)(2,1)}, u32[]{:S(2)}) copy-start(bf16[64,2,2048]{2,1,0:T(2,128)(2,1)} %param.14) | copy-start | bytes 1572868
  574.4 36.0 %all-to-all-start.1 = ((bf16[128,4,2048]{2,1,0:T(4,128)(2,1)}), bf16[128,4,2048]{2,1,0:T(4,128)(2,1)}, u32[]{:S(2)}, u32[]{:S(2)}) async-start(bf16[128,4,2048]{2,1,0:T(4,128)(2,1)} %reshape.145), calls=%async_computation.2 | async-start | bytes 4194304 | tf_op jit(solution)/shard_map/all_to_all | solution.py:154
Sparse Core Ops, SparseCore 0:
  68.5 81.9 all-gather.2
  152.6 77.6 all-gather.4
  464.8 35.5 reduce-scatter.1
